TPU v7x, 32 devices: a whole 2x2x4 slice. The times are simulated.
32 devices in a mesh: groups: 2 (over y), tensor: 4 (over z), store: 4 (over x, core).
Axes of the slice: x: 2, y: 2, z: 4, core: 2. Of those that a mesh axis runs over, the one named last changes fastest.
Arguments:
- tokens: bfloat16 [4096, 8192], P(('groups', 'store', 'tensor')), parts along dimension 0, may hold values from -32 to 32
- query_weight: bfloat16 [8192, 8192], P(None, 'tensor'), may hold values from -0.0625 to 0.0625
- key_value_weight: bfloat16 [8192, 2048], P(None, 'tensor'), may hold values from -0.0625 to 0.0625
- adapter_down_maps: bfloat16 [32, 128, 8192], P('store', None, 'tensor'), may hold values from -0.0625 to 0.0625
- adapter_up_query: bfloat16 [32, 64, 8192], P('store', None, 'tensor'), may hold values from -0.375 to 0.375
- adapter_up_key_value: bfloat16 [32, 64, 2048], P('store', None, 'tensor'), may hold values from -0.375 to 0.375
- adapter_row_table: int32 [64], P('groups'), parts along dimension 0, may hold values from 0 to 31, as said below
- request_adapter_ids: int32 [8, 4], P('groups'), parts along dimension 0, may hold values from 0 to 31, as said below
- token_request_ids: int32 [8, 512], P(('groups', 'store')), parts along dimension 0, may hold values from 0 to 3, never falling along the last dimension, each value on 1 to 256 neighbouring positions
Outputs:
- attention: bfloat16 [4096, 8192], P(('groups', 'store'), 'tensor'), parts along dimension 0
There are 2 independent parts, one for each index of `groups`. A program takes and returns all parts, laid end to end along the dimension named above; an argument that names none is the same for every part. Nothing has to cross between parts.
Inputs may be any that keep to these rules, and one draw needn't show every extreme that they name: A permutation: adapter a lies in row adapter_row_table[a] of the adapter arrays, on store index adapter_row_table[a] // 8. `request_adapter_ids`: the 4 requests of one store batch use adapters held on 4 different store indices. `token_request_ids`: requests are contiguous runs of a store batch, each of 1 to 256 tokens.
All inputs are finite; a program needn't handle non-finite values.
Results may differ from a plain program's by a relative error of at most 0.012.
The roundings to bfloat16 on the way count: a program that leaves them out, or rounds other values in their place, can miss the bound.
Values may be sent and summed in bfloat16 or wider, within the bound.
A program may use at most 128 MiB of HBM per device.

v0:
```python
import math
import jax
import jax.numpy as jnp
from jax import lax
from jax.sharding import PartitionSpec as P

MODEL_WIDTH = 8192
QUERY_HEADS = 64
KEY_VALUE_HEADS = 8
HEAD_SIZE = 128
ADAPTER_RANK = 64
STORE_REQUESTS = 4
TOK_ST = 512
adapter_scale = 2.0
rope_theta = 500000.0


def from_partner(shard, axis, bit):
    return lax.ppermute(shard, axis, [(i, i ^ 1 << bit) for i in range(lax.axis_size(axis))])


def token_positions(segment_row):
    members = segment_row[:, None] == jnp.arange(STORE_REQUESTS, dtype=jnp.int32)[None, :]
    counts = jnp.sum(members.astype(jnp.int32), axis=0)
    starts = jnp.cumsum(counts) - counts
    first_index = jnp.sum(jnp.where(members, starts[None, :], 0), axis=1)
    return jnp.arange(segment_row.shape[0], dtype=jnp.int32) - first_index


def rotary(heads_values, positions):
    half_size = heads_values.shape[-1] // 2
    exponent = jnp.arange(half_size, dtype=jnp.float32) * (2.0 / heads_values.shape[-1])
    frequency = jnp.exp(-exponent * math.log(rope_theta))
    angles = positions.astype(jnp.float32)[:, None] * frequency[None, :]
    cosine = jnp.cos(angles)[:, None, :]
    sine = jnp.sin(angles)[:, None, :]
    lower = heads_values[..., :half_size]
    upper = heads_values[..., half_size:]
    return jnp.concatenate([lower * cosine - upper * sine, upper * cosine + lower * sine], axis=-1)


def select_rows(selector, stack):
    flat = stack.reshape(stack.shape[0], -1)
    picked = jnp.dot(selector, flat, preferred_element_type=jnp.float32)
    return picked.reshape(selector.shape[:-1] + stack.shape[1:])


def on_device(
    tokens,
    query_weight,
    key_value_weight,
    adapter_down_maps,
    adapter_up_query,
    adapter_up_key_value,
    adapter_row_table,
    request_adapter_ids,
    token_request_ids,
):
    tensor_rank = lax.axis_index("tensor")
    store_rank = lax.axis_index("store")
    tensor_count = lax.axis_size("tensor")
    store_count = lax.axis_size("store")
    position_count = adapter_down_maps.shape[0]
    adapter_total = adapter_row_table.shape[0]
    lookup = (
        request_adapter_ids[:, :, None] == jnp.arange(adapter_total, dtype=jnp.int32)[None, None, :]
    ).astype(jnp.int32)
    slot_table = jnp.sum(lookup * adapter_row_table[None, None, :], axis=2)
    my_slots = lax.dynamic_index_in_dim(slot_table, store_rank, 0, keepdims=False)
    local_slots = store_rank * position_count + jnp.arange(position_count, dtype=jnp.int32)
    serving = jnp.sum(
        (slot_table[:, :, None] == local_slots[None, None, :]).astype(jnp.int32), axis=1
    ).astype(jnp.bfloat16)
    out_down = select_rows(serving, adapter_down_maps).astype(jnp.bfloat16)
    out_query = select_rows(serving, adapter_up_query).astype(jnp.bfloat16)
    out_keyval = select_rows(serving, adapter_up_key_value).astype(jnp.bfloat16)
    got_down, got_query, got_keyval = (
        lax.all_to_all(out_down, "store", split_axis=0, concat_axis=0, tiled=True),
        lax.all_to_all(out_query, "store", split_axis=0, concat_axis=0, tiled=True),
        lax.all_to_all(out_keyval, "store", split_axis=0, concat_axis=0, tiled=True),
    )
    holder_pick = (
        (my_slots // position_count)[:, None] == jnp.arange(store_count, dtype=jnp.int32)[None, :]
    ).astype(jnp.bfloat16)
    down_blocks = select_rows(holder_pick, got_down).astype(jnp.bfloat16)
    up_query_blocks = select_rows(holder_pick, got_query).astype(jnp.bfloat16)
    up_keyval_blocks = select_rows(holder_pick, got_keyval).astype(jnp.bfloat16)
    segment_row = token_request_ids[0]
    members = segment_row[:, None] == jnp.arange(STORE_REQUESTS, dtype=jnp.int32)[None, :]
    member_float = members.astype(jnp.float32)
    member_half = members.astype(jnp.bfloat16)
    width_share = MODEL_WIDTH // tensor_count
    column_first = tensor_rank * width_share
    down_matrix = down_blocks.reshape(STORE_REQUESTS * 2 * ADAPTER_RANK, width_share)
    query_width = query_weight.shape[1]
    keyval_width = key_value_weight.shape[1]
    rows_piece = lax.all_gather(tokens, "tensor", axis=0, tiled=True)
    count = rows_piece.shape[0]
    plain_query = jnp.dot(rows_piece, query_weight, preferred_element_type=jnp.float32)
    plain_key_value = jnp.dot(rows_piece, key_value_weight, preferred_element_type=jnp.float32)
    features = lax.dynamic_slice_in_dim(rows_piece, column_first, width_share, 1)
    partial_low = lax.dot_general(
        features, down_matrix, (((1,), (1,)), ((), ())), preferred_element_type=jnp.float32
    )
    partial_low = jnp.sum(
        partial_low.reshape(count, STORE_REQUESTS, 2 * ADAPTER_RANK) * member_float[:, :, None],
        axis=1,
    )
    joined = jnp.concatenate([plain_query, plain_key_value, partial_low], axis=1)
    plain_query = joined[:, :query_width]
    plain_key_value = joined[:, query_width : query_width + keyval_width]
    low = lax.psum(joined[:, query_width + keyval_width :], "tensor").astype(jnp.bfloat16)
    token_query_update = (low[:, None, :ADAPTER_RANK] * member_half[:, :, None]).reshape(
        TOK_ST, STORE_REQUESTS * ADAPTER_RANK
    )
    token_key_value_update = (low[:, None, ADAPTER_RANK:] * member_half[:, :, None]).reshape(
        TOK_ST, STORE_REQUESTS * ADAPTER_RANK
    )
    query_update = jnp.dot(
        token_query_update,
        up_query_blocks.reshape(STORE_REQUESTS * ADAPTER_RANK, query_width),
        preferred_element_type=jnp.float32,
    )
    key_value_update = jnp.dot(
        token_key_value_update,
        up_keyval_blocks.reshape(STORE_REQUESTS * ADAPTER_RANK, keyval_width),
        preferred_element_type=jnp.float32,
    )
    query_unrotated = plain_query + adapter_scale * query_update
    key_value_unrotated = plain_key_value + adapter_scale * key_value_update
    positions = token_positions(segment_row)
    head_local = query_width // HEAD_SIZE
    query = rotary(query_unrotated.reshape(TOK_ST, head_local, HEAD_SIZE), positions).astype(
        jnp.bfloat16
    )
    pair_heads = keyval_width // HEAD_SIZE
    keyval_heads = key_value_unrotated.reshape(TOK_ST, pair_heads, HEAD_SIZE)
    holds_keys = tensor_rank % 2 == 0
    own_part = jnp.where(holds_keys, rotary(keyval_heads, positions), keyval_heads).astype(
        jnp.bfloat16
    )
    other_part = from_partner(own_part, "tensor", 0)
    keys = jnp.where(holds_keys, own_part, other_part)
    values = jnp.where(holds_keys, other_part, own_part)
    group_size = QUERY_HEADS // KEY_VALUE_HEADS
    kv_used = max(head_local // group_size, 1)
    per_kv = head_local // kv_used
    kv_first = tensor_rank * head_local // group_size - tensor_rank // 2 * pair_heads
    keys_used = lax.dynamic_slice_in_dim(keys, kv_first, kv_used, 1)
    values_used = lax.dynamic_slice_in_dim(values, kv_first, kv_used, 1)
    grouped = query.reshape(TOK_ST, kv_used, per_kv, HEAD_SIZE)
    scores = jnp.einsum(
        "tkgd,skd->kgts", grouped, keys_used, preferred_element_type=jnp.float32
    ) / math.sqrt(HEAD_SIZE)
    token_index = jnp.arange(TOK_ST, dtype=jnp.int32)
    allowed = (segment_row[:, None] == segment_row[None, :]) & (
        token_index[:, None] >= token_index[None, :]
    )
    scores = jnp.where(allowed, scores, -1e30)
    scores = scores - jnp.max(scores, axis=-1, keepdims=True)
    weights = jnp.exp(scores)
    weights = (weights / jnp.sum(weights, axis=-1, keepdims=True)).astype(jnp.bfloat16)
    mixed = jnp.einsum("kgts,skd->tkgd", weights, values_used, preferred_element_type=jnp.float32)
    return mixed.reshape(TOK_ST, query_width).astype(jnp.bfloat16)


def solution(mesh):
    return jax.shard_map(
        on_device,
        mesh=mesh,
        in_specs=(
            P(("groups", "store", "tensor"), None),
            P(None, "tensor"),
            P(None, "tensor"),
            P("store", None, "tensor"),
            P("store", None, "tensor"),
            P("store", None, "tensor"),
            P("groups"),
            P("groups", None),
            P(("groups", "store"), None),
        ),
        out_specs=P(("groups", "store"), "tensor"),
        check_vma=False,
    )
```

profile of v0, /device:TPU:0, one launch (start us, length us, event | category | flops | bytes accessed | tf_op | source)
XLA Modules:
  0.0 270.4 jit_solution(15919129932199313101)
XLA Ops:
  6.5 0.0 copy-start
  6.5 0.0 all-gather.2.cloned.1.call-start
  6.5 0.7 all-gather.2.cloned.1.call-update
  7.3 0.9 select_reduce_fusion.1
  8.2 0.1 convert_reduce_fusion.1
  8.3 1.4 convolution_convert_fusion.4
  9.7 0.0 copy-start.4
  9.7 0.7 copy.34
  10.5 4.2 %all-to-all-start.1 = ((bf16[4,64,512]{2,1,0:T(8,128)(2,1)}), bf16[4,64,512]{2,1,0:T(8,128)(2,1)S(1)}, u32[]{:S(2)}, u32[]{:S(2)}) async-start(bf16[4,64,512]{2,1,0:T(8,128)(2,1)} %copy.34), calls=%async_computation.1 | async-start | bytes 524288 | tf_op jit(solution)/shard_map/all_to_all | solution.py:80
  14.7 0.0 copy-done
  14.7 1.6 convolution_convert_fusion.3
  16.3 1.6 copy.40
  18.0 2.8 %all-to-all-done.1 = bf16[4,64,512]{2,1,0:T(8,128)(2,1)S(1)} async-done(((bf16[4,64,512]{2,1,0:T(8,128)(2,1)}), bf16[4,64,512]{2,1,0:T(8,128)(2,1)S(1)}, u32[]{:S(2)}, u32[]{:S(2)}) %all-to-all-start.1) | async-done | bytes 262176 | tf_op jit(solution)/shard_map/all_to_all | solution.py:80
  20.7 3.5 %all-to-all-start.2 = ((bf16[4,64,2048]{2,1,0:T(8,128)(2,1)}), bf16[4,64,2048]{2,1,0:T(8,128)(2,1)S(1)}, u32[]{:S(2)}, u32[]{:S(2)}) async-start(bf16[4,64,2048]{2,1,0:T(8,128)(2,1)} %copy.40), calls=%async_computation.2 | async-start | bytes 2097152 | tf_op jit(solution)/shard_map/all_to_all | solution.py:79
  24.3 0.0 copy-done.4
  24.3 0.1 convert_reduce_fusion
  24.4 0.2 reduce-window.8
  24.6 5.4 %convolution_convert_fusion = bf16[4,128,2048]{2,0,1:T(4,128)(2,1)S(1)} fusion(s32[4,8]{1,0:T(4,128)S(1)} %convert_reduce_fusion.1, bf16[1,8,128,2048]{3,2,1,0:T(8,128)(2,1)} %bitcast.125), kind=kOutput, calls=%fused_computation.14 | convolution fusion | flops 17825824 | bytes 6291584 | tf_op jit(solution)/shard_map/dot_general | solution.py:44
  30.0 2.5 copy.31
  32.5 6.2 %all-to-all-done.2 = bf16[4,64,2048]{2,1,0:T(8,128)(2,1)S(1)} async-done(((bf16[4,64,2048]{2,1,0:T(8,128)(2,1)}), bf16[4,64,2048]{2,1,0:T(8,128)(2,1)S(1)}, u32[]{:S(2)}, u32[]{:S(2)}) %all-to-all-start.2) | async-done | bytes 1048608 | tf_op jit(solution)/shard_map/all_to_all | solution.py:79
  38.7 0.0 copy-start.2
  38.7 1.0 copy-done.2
  39.7 3.8 %all-to-all-start = ((bf16[4,128,2048]{2,1,0:T(8,128)(2,1)}), bf16[4,128,2048]{2,1,0:T(8,128)(2,1)S(1)}, u32[]{:S(2)}, u32[]{:S(2)}) async-start(bf16[4,128,2048]{2,1,0:T(8,128)(2,1)} %copy.31), calls=%async_computation | async-start | bytes 4194304 | tf_op jit(solution)/shard_map/all_to_all | solution.py:78
  43.5 0.1 select_reduce_fusion
  43.6 0.2 fusion.31
  43.8 1.0 multiply_cosine_fusion
  44.8 0.4 convolution_convert_fusion.5
  45.2 3.3 %convolution_convert_fusion.2 = bf16[4,64,2048]{2,0,1:T(4,128)(2,1)} fusion(s32[4]{0:T(128)S(1)} %and_select_fusion, bf16[1,4,64,2048]{3,2,1,0:T(8,128)(2,1)} %bitcast.129), kind=kOutput, calls=%fused_computation.16 | convolution fusion | flops 4718608 | bytes 2097168 | tf_op jit(solution)/shard_map/dot_general | solution.py:44
  48.4 20.5 %all-to-all-done = bf16[4,128,2048]{2,1,0:T(8,128)(2,1)S(1)} async-done(((bf16[4,128,2048]{2,1,0:T(8,128)(2,1)}), bf16[4,128,2048]{2,1,0:T(8,128)(2,1)S(1)}, u32[]{:S(2)}, u32[]{:S(2)}) %all-to-all-start) | async-done | bytes 2097184 | tf_op jit(solution)/shard_map/all_to_all | solution.py:78
  68.9 3.1 %convolution_convert_fusion.1 = bf16[4,128,2048]{2,0,1:T(4,128)(2,1)} fusion(s32[4]{0:T(128)S(1)} %and_select_fusion, bf16[1,4,128,2048]{3,2,1,0:T(8,128)(2,1)S(1)} %bitcast.127), kind=kOutput, calls=%fused_computation.15 | convolution fusion | flops 9437200 | bytes 4194320 | tf_op jit(solution)/shard_map/dot_general | solution.py:44
  72.0 89.3 %all-gather.2.cloned.1.call-done = bf16[512,8192]{1,0:T(8,128)(2,1)} async-done(((bf16[128,8192]{1,0:T(8,128)(2,1)}), bf16[512,8192]{1,0:T(8,128)(2,1)}) %all-gather.2.cloned.1.call-update) | async-done | bytes 8388624 | tf_op jit(solution)/shard_map/all_gather | solution.py:97
  161.3 4.9 %fusion.24 = f32[512,128]{1,0:T(8,128)S(1)} fusion(bf16[4,128,2048]{2,0,1:T(4,128)(2,1)} %convolution_convert_fusion.1, bf16[512,8192]{1,0:T(8,128)(2,1)} %all-gather.2.cloned.1.call-done, s32[]{:T(128)S(6)} %select_n.62, f32[512,4]{0,1:T(4,128)S(1)} %get-tuple-element.14), kind=kOutput, calls=%fused_computation.31 | convolution fusion | flops 1074200576 | bytes 4464644 | tf_op jit(solution)/shard_map/dot_general | solution.py:102
  166.2 21.4 %all-reduce.1 = bf16[512,128]{1,0:T(8,128)(2,1)S(1)} all-reduce(f32[512,128]{1,0:T(8,128)S(1)} %fusion.24), channel_id=1, replica_groups=mesh['groups'=2,'tensor'=4,'store'=4] {'tensor'}, use_global_device_ids=true, to_apply=%region_3.4 | all-reduce | flops 65536 | bytes 393216 | tf_op jit(solution)/shard_map/psum | solution.py:112
  187.6 0.1 fusion.68
  187.7 0.1 copy.33
  187.8 9.5 %fusion.82 = f32[512,512]{0,1:T(8,128)S(1)} fusion(bf16[512,8192]{1,0:T(8,128)(2,1)} %all-gather.2.cloned.1.call-done, bf16[8192,512]{1,0:T(8,128)(2,1)} %param.11), kind=kOutput, calls=%fused_computation.106 | convolution fusion | flops 4294967296 | bytes 17825792 | tf_op jit(solution)/shard_map/dot_general | solution.py:100
  197.3 0.3 fusion.23
  197.6 0.3 copy.36
  197.9 0.1 copy.39
  198.1 0.4 multiply_subtract_fusion
  198.5 0.3 fusion.29
  198.8 0.0 copy-start.1
  198.8 0.1 collective-permute-start
  198.9 23.8 %fusion.83 = f32[512,2048]{1,0:T(8,128)S(1)} fusion(bf16[512,8192]{1,0:T(8,128)(2,1)} %all-gather.2.cloned.1.call-done, bf16[8192,2048]{1,0:T(8,128)(2,1)} %param.10), kind=kOutput, calls=%fused_computation.107 | convolution fusion | flops 17179869184 | bytes 46137344 | tf_op jit(solution)/shard_map/dot_general | solution.py:99
  222.8 0.0 copy-done.1
  222.8 1.7 fusion.7
  224.5 0.9 copy.58
  225.5 1.8 subtract_convert_fusion
  227.3 0.5 copy.42
  227.9 0.5 copy.43
  228.4 0.0 collective-permute-done
  228.4 0.0 copy-start.3
  228.4 8.2 %fusion.8 = f32[2,512,512,8]{2,1,3,0:T(8,128)} fusion(bf16[512,2,8,64]{3,0,2,1:T(8,128)(2,1)S(1)} %bitcast.123, bf16[512,2,8,64]{3,0,2,1:T(8,128)(2,1)S(1)} %bitcast.122, pred[]{:T(512)S(6)} %eq.43, bf16[512,4,128]{2,0,1:T(8,128)(2,1)S(1)} %fusion.29, s32[]{:T(128)S(6)} %select_n.70, bf16[512,4,128]{2,0,1:T(8,128)(2,1)S(1)} %collective-permute-done), kind=kOutput, calls=%fused_computation.18 | convolution fusion | flops 1078067200 | bytes 21495812 | tf_op jit(solution)/shard_map/tkgd,skd->kgts/dot_general | solution.py:152
  236.6 0.0 copy-done.3
  236.6 17.2 %fusion.69 = (f32[2,8,512]{2,1,0:T(8,128)S(1)}, f32[2,8,512,512]{2,3,1,0:T(8,128)}) fusion(f32[2,512,512,8]{2,1,3,0:T(8,128)} %fusion.8, pred[512,512]{0,1:T(8,128)(4,1)S(1)} %fusion.31), kind=kOutput, calls=%fused_computation.93 | output fusion | flops 25166336 | bytes 33849344 | tf_op jit(solution)/shard_map/sub | solution.py:160
  253.8 7.3 %fusion.16 = bf16[2,128,8,512]{3,1,2,0:T(8,128)(2,1)S(1)} fusion(f32[2,8,512,512]{2,3,1,0:T(8,128)} %get-tuple-element.16, f32[2,8,512]{2,1,0:T(8,128)S(1)} %get-tuple-element.15, pred[]{:T(512)S(6)} %eq.43, bf16[512,4,128]{2,0,1:T(8,128)(2,1)S(1)} %fusion.29, s32[]{:T(128)S(6)} %select_n.70, bf16[512,4,128]{2,0,1:T(8,128)(2,1)} %copy-done.3), kind=kOutput, calls=%fused_computation.26 | convolution fusion | flops 1083310080 | bytes 19431428 | tf_op jit(solution)/shard_map/kgts,skd->tkgd/dot_general | solution.py:163
  261.2 2.4 copy.46
  (6 shorter events, 0.0 us)
Async XLA Ops:
  6.5 8.2 %copy-start = (bf16[8,64,2048]{2,1,0:T(8,128)(2,1)S(1)}, bf16[8,64,2048]{2,1,0:T(8,128)(2,1)}, u32[]{:S(2)}) copy-start(bf16[8,64,2048]{2,1,0:T(8,128)(2,1)} %param.13) | copy-start | bytes 6291460
  6.5 154.7 %all-gather.2.cloned.1.call-start = ((), (), s32[]{:S(2)}) async-start(), calls=%async_computation.3 | async-start | bytes 10485760 | tf_op jit(solution)/shard_map/all_gather | solution.py:97
  9.7 14.6 %copy-start.4 = (s32[1,512]{1,0:T(1,128)S(1)}, s32[1,512]{1,0:T(1,128)}, u32[]{:S(2)}) copy-start(s32[1,512]{1,0:T(1,128)} %param.17) | copy-start | bytes 6148
  10.5 10.2 %all-to-all-start.1 = ((bf16[4,64,512]{2,1,0:T(8,128)(2,1)}), bf16[4,64,512]{2,1,0:T(8,128)(2,1)S(1)}, u32[]{:S(2)}, u32[]{:S(2)}) async-start(bf16[4,64,512]{2,1,0:T(8,128)(2,1)} %copy.34), calls=%async_computation.1 | async-start | bytes 524288 | tf_op jit(solution)/shard_map/all_to_all | solution.py:80
  20.7 17.9 %all-to-all-start.2 = ((bf16[4,64,2048]{2,1,0:T(8,128)(2,1)}), bf16[4,64,2048]{2,1,0:T(8,128)(2,1)S(1)}, u32[]{:S(2)}, u32[]{:S(2)}) async-start(bf16[4,64,2048]{2,1,0:T(8,128)(2,1)} %copy.40), calls=%async_computation.2 | async-start | bytes 2097152 | tf_op jit(solution)/shard_map/all_to_all | solution.py:79
  38.7 1.0 copy-start.2
  39.7 29.3 %all-to-all-start = ((bf16[4,128,2048]{2,1,0:T(8,128)(2,1)}), bf16[4,128,2048]{2,1,0:T(8,128)(2,1)S(1)}, u32[]{:S(2)}, u32[]{:S(2)}) async-start(bf16[4,128,2048]{2,1,0:T(8,128)(2,1)} %copy.31), calls=%async_computation | async-start | bytes 4194304 | tf_op jit(solution)/shard_map/all_to_all | solution.py:78
  198.8 23.9 %copy-start.1 = (bf16[4,64,2048]{2,0,1:T(4,128)(2,1)S(1)}, bf16[4,64,2048]{2,0,1:T(4,128)(2,1)}, u32[]{:S(2)}) copy-start(bf16[4,64,2048]{2,0,1:T(4,128)(2,1)} %convolution_convert_fusion.2) | copy-start | bytes 3145732
  198.8 29.6 %collective-permute-start = (bf16[512,4,128]{2,0,1:T(8,128)(2,1)S(1)}, bf16[512,4,128]{2,0,1:T(8,128)(2,1)S(1)}, u32[]{:S(2)}, u32[]{:S(2)}) collective-permute-start(bf16[512,4,128]{2,0,1:T(8,128)(2,1)S(1)} %fusion.29), channel_id=1, source_target_pairs={{0,4},{4,0},{8,12},{12,8},{1,5},{5,1},{9,13},{13,9},{2,6},{6,2},{1... | collective-permute-start | bytes 1572872 | tf_op jit(solution)/shard_map/ppermute | solution.py:19
  228.4 8.2 %copy-start.3 = (bf16[512,4,128]{2,0,1:T(8,128)(2,1)}, bf16[512,4,128]{2,0,1:T(8,128)(2,1)S(1)}, u32[]{:S(2)}) copy-start(bf16[512,4,128]{2,0,1:T(8,128)(2,1)S(1)} %collective-permute-done) | copy-start | bytes 1572868
Sparse Core Ops, SparseCore 0:
  8.9 152.3 all-gather.1
where the time goes:
time: 271 us; the launch traced here: 270 us
  waiting for transfers between devices  119 us (44%)
  matrix products  71 us (26%)
  other arithmetic  22.4 us (8%)
  blocking collectives  21.4 us (8%)
  between operations  13.7 us (5%)
  starting transfers between devices  11.6 us (4%)
  local copies, waits for them, and re-layouts  10.9 us (4%)
    all_gather x1, waiting for transfers between devices, on_device(): rows_piece = lax.all_gather(tokens, 'tensor', axis=0, tiled=True)  89.3 us
    dot_general x1, matrix products, on_device(): jnp.dot(rows_piece, query_weight, preferred_element_type=jnp.float32)  23.8 us
    psum x1, blocking collectives, on_device(): lax.psum(joined[:, query_width + keyval_width:], 'tensor')  21.4 us
    all_to_all x1, waiting for transfers between devices, on_device(): lax.all_to_all(out_down, 'store', split_axis=0, concat_axis=0, tiled=True)  20.5 us
    sub x1, other arithmetic, on_device(): scores = scores - jnp.max(scores, axis=-1, keepdims=True)  17.2 us
    dot_general x6, matrix products, select_rows(): picked = jnp.dot(selector, flat, preferred_element_type=jnp.float32)  15.1 us
    dot_general x1, matrix products, on_device(): jnp.dot(rows_piece, key_value_weight, preferred_element_type=jnp.float32)  9.46 us
    dot_general x1, matrix products, on_device(): jnp.einsum('tkgd,skd->kgts', grouped, keys_used, preferred_element_type=j...  8.15 us
  transfers between devices with their start and end apart: 5, of which 4 were waited for; matrix products, arithmetic and copies ran while one was open for 19% of the time, Pallas kernels for 0%

commit v1 on v0

--- a/solution.py
+++ b/solution.py
@@ -94,7 +94,9 @@
     down_matrix = down_blocks.reshape(STORE_REQUESTS * 2 * ADAPTER_RANK, width_share)
     query_width = query_weight.shape[1]
     keyval_width = key_value_weight.shape[1]
-    rows_piece = lax.all_gather(tokens, "tensor", axis=0, tiled=True)
+    rows_piece = jnp.concatenate(
+        lax.all_to_all(jnp.stack([tokens] * lax.axis_size("tensor")), "tensor", 0, 0), axis=0
+    )
     count = rows_piece.shape[0]
     plain_query = jnp.dot(rows_piece, query_weight, preferred_element_type=jnp.float32)
     plain_key_value = jnp.dot(rows_piece, key_value_weight, preferred_element_type=jnp.float32)

time: 271 us -> 362 us (1.34)
  waiting for transfers between devices: 119 us -> 186 us
  blocking collectives: 21.4 us -> 51.1 us
  between operations: 13.7 us -> 0.28 us
    all_to_all x1, waiting for transfers between devices: 20.5 us -> 175 us  [on_device(): lax.all_to_all(jnp.stack([tokens] * lax.axis_size('tensor')), 'tensor', 0...]
    all_gather x1 -> x0, waiting for transfers between devices: 89.3 us -> none  [on_device(): rows_piece = lax.all_gather(tokens, 'tensor', axis=0, tiled=True)]
    all_to_all x0 -> x1, blocking collectives: none -> 29.1 us  [on_device(): lax.all_to_all(out_down, 'store', split_axis=0, concat_axis=0, tiled=True)]
    another operation x2 -> x3, local copies, waits for them, and re-layouts: 1.08 us -> 5.49 us  [the longest x1 4.41 us: on_device(): jnp.stack([tokens] * lax.axis_size('tensor'))]
  transfers between devices with their start and end apart: 5 -> 4, of which waited for: 4 -> 4; matrix products, arithmetic and copies ran while one was open for 19% -> 7% of each run, Pallas kernels for 0% -> 0%
where the time goes in v1:
time: 362 us
  waiting for transfers between devices  186 us (51%)
  matrix products  73.2 us (20%)
  blocking collectives  51.1 us (14%)
  other arithmetic  23.1 us (6%)
  local copies, waits for them, and re-layouts  14.5 us (4%)
  starting transfers between devices  13.8 us (4%)
    all_to_all x1, waiting for transfers between devices, on_device(): lax.all_to_all(jnp.stack([tokens] * lax.axis_size('tensor')), 'tensor', 0...  175 us
    all_to_all x1, blocking collectives, on_device(): lax.all_to_all(out_down, 'store', split_axis=0, concat_axis=0, tiled=True)  29.1 us
    dot_general x1, matrix products, on_device(): jnp.dot(rows_piece, query_weight, preferred_element_type=jnp.float32)  24.8 us
    psum x1, blocking collectives, on_device(): lax.psum(joined[:, query_width + keyval_width:], 'tensor')  21.9 us
    sub x1, other arithmetic, on_device(): scores = scores - jnp.max(scores, axis=-1, keepdims=True)  17.2 us
    dot_general x6, matrix products, select_rows(): picked = jnp.dot(selector, flat, preferred_element_type=jnp.float32)  16.5 us
    dot_general x1, matrix products, on_device(): jnp.dot(rows_piece, key_value_weight, preferred_element_type=jnp.float32)  9.46 us
    dot_general x1, matrix products, on_device(): jnp.einsum('tkgd,skd->kgts', grouped, keys_used, preferred_element_type=j...  8.15 us
  transfers between devices with their start and end apart: 4, of which 4 were waited for; matrix products, arithmetic and copies ran while one was open for 7% of the time, Pallas kernels for 0%

profile of v1, /device:TPU:0, one launch (start us, length us, event | category | flops | bytes accessed | tf_op | source)
XLA Modules:
  0.0 361.7 jit_solution(13655176128828658042)
XLA Ops:
  0.0 0.9 select_reduce_fusion.1
  0.9 0.1 convert_reduce_fusion.1
  1.0 1.4 convolution_convert_fusion.4
  2.5 0.7 copy.34
  3.2 4.2 %all-to-all-start.2 = ((bf16[4,64,512]{2,1,0:T(8,128)(2,1)}), bf16[4,64,512]{2,1,0:T(8,128)(2,1)S(1)}, u32[]{:S(2)}, u32[]{:S(2)}) async-start(bf16[4,64,512]{2,1,0:T(8,128)(2,1)} %copy.34), calls=%async_computation.2 | async-start | bytes 524288 | tf_op jit(solution)/shard_map/all_to_all | solution.py:80
  7.4 3.2 convolution_convert_fusion.3
  10.6 1.5 copy.40
  12.2 1.3 all-to-all-done.2
  13.4 3.5 all-to-all-start.3
  17.0 5.3 %convolution_convert_fusion = bf16[4,128,2048]{2,0,1:T(4,128)(2,1)S(1)} fusion(s32[4,8]{1,0:T(4,128)S(1)} %convert_reduce_fusion.1, bf16[1,8,128,2048]{3,2,1,0:T(8,128)(2,1)} %bitcast.126), kind=kOutput, calls=%fused_computation.14 | convolution fusion | flops 17825824 | bytes 6291584 | tf_op jit(solution)/shard_map/dot_general | solution.py:44
  22.3 1.2 copy.31
  23.4 7.9 %all-to-all-done.3 = bf16[4,64,2048]{2,1,0:T(8,128)(2,1)S(1)} async-done(((bf16[4,64,2048]{2,1,0:T(8,128)(2,1)}), bf16[4,64,2048]{2,1,0:T(8,128)(2,1)S(1)}, u32[]{:S(2)}, u32[]{:S(2)}) %all-to-all-start.3) | async-done | bytes 1048608 | tf_op jit(solution)/shard_map/all_to_all | solution.py:79
  31.4 0.0 copy-start.4
  31.4 0.0 copy-start.1
  31.4 29.1 %all_to_all.20 = bf16[4,128,2048]{2,1,0:T(8,128)(2,1)} all-to-all(bf16[4,128,2048]{2,1,0:T(8,128)(2,1)S(1)} %copy.31), channel_id=1, replica_groups=mesh['groups'=2,'tensor'=4,'store'=4] {'store'}, dimensions={0} | all-to-all | bytes 4194304 | tf_op jit(solution)/shard_map/all_to_all | solution.py:78
  60.5 0.0 copy-done.1
  60.5 4.4 %stack.2 = bf16[4,128,8192]{2,1,0:T(8,128)(2,1)} broadcast(bf16[128,8192]{1,0:T(8,128)(2,1)S(1)} %copy-done.1), dimensions={1,2} | broadcast | bytes 10485760 | tf_op jit(solution)/shard_map/stack | solution.py:98
  64.9 0.0 copy-done.4
  64.9 0.0 copy-start.6
  64.9 0.0 copy-start.2
  64.9 6.0 %all-to-all-start = ((bf16[4,128,8192]{2,1,0:T(8,128)(2,1)}), bf16[4,128,8192]{2,1,0:T(8,128)(2,1)}, u32[]{:S(2)}, u32[]{:S(2)}) async-start(bf16[4,128,8192]{2,1,0:T(8,128)(2,1)} %stack.2), calls=%async_computation | async-start | bytes 16777216 | tf_op jit(solution)/shard_map/all_to_all | solution.py:98
  70.9 0.0 copy-done.6
  71.0 0.1 convert_reduce_fusion
  71.1 0.2 reduce-window.8
  71.3 0.1 select_reduce_fusion
  71.4 0.9 fusion.31
  72.3 1.0 multiply_cosine_fusion
  73.3 0.4 convolution_convert_fusion.5
  73.7 3.2 convolution_convert_fusion.2
  76.8 0.0 copy-done.2
  76.8 3.1 convolution_convert_fusion.1
  79.9 174.5 %all-to-all-done = bf16[4,128,8192]{2,1,0:T(8,128)(2,1)} async-done(((bf16[4,128,8192]{2,1,0:T(8,128)(2,1)}), bf16[4,128,8192]{2,1,0:T(8,128)(2,1)}, u32[]{:S(2)}, u32[]{:S(2)}) %all-to-all-start) | async-done | bytes 8388640 | tf_op jit(solution)/shard_map/all_to_all | solution.py:98
  254.5 4.9 %fusion.24 = f32[512,128]{1,0:T(8,128)S(1)} fusion(bf16[4,128,2048]{2,0,1:T(4,128)(2,1)} %convolution_convert_fusion.1, bf16[512,8192]{1,0:T(8,128)(2,1)} %bitcast, s32[]{:T(128)S(6)} %select_n.62, f32[512,4]{0,1:T(4,128)S(1)} %get-tuple-element.14), kind=kOutput, calls=%fused_computation.31 | convolution fusion | flops 1074200576 | bytes 4464644 | tf_op jit(solution)/shard_map/dot_general | solution.py:104
  259.4 21.9 %all-reduce.1 = bf16[512,128]{1,0:T(8,128)(2,1)S(1)} all-reduce(f32[512,128]{1,0:T(8,128)S(1)} %fusion.24), channel_id=1, replica_groups=mesh['groups'=2,'tensor'=4,'store'=4] {'tensor'}, use_global_device_ids=true, to_apply=%region_3.4 | all-reduce | flops 65536 | bytes 393216 | tf_op jit(solution)/shard_map/psum | solution.py:114
  281.4 0.1 fusion.68
  281.5 0.1 copy.33
  281.6 0.1 copy.39
  281.7 9.5 %fusion.82 = f32[512,512]{0,1:T(8,128)S(1)} fusion(bf16[512,8192]{1,0:T(8,128)(2,1)} %bitcast, bf16[8192,512]{1,0:T(8,128)(2,1)} %param.11), kind=kOutput, calls=%fused_computation.106 | convolution fusion | flops 4294967296 | bytes 17825792 | tf_op jit(solution)/shard_map/dot_general | solution.py:102
  291.1 24.8 %fusion.83 = f32[512,2048]{1,0:T(8,128)} fusion(bf16[512,8192]{1,0:T(8,128)(2,1)} %bitcast, bf16[8192,2048]{1,0:T(8,128)(2,1)} %param.10), kind=kOutput, calls=%fused_computation.107 | convolution fusion | flops 17179869184 | bytes 46137344 | tf_op jit(solution)/shard_map/dot_general | solution.py:101
  316.0 0.3 fusion.23
  316.3 0.3 copy.36
  316.7 0.0 copy-start
  316.7 0.0 copy-start.3
  316.7 0.4 multiply_subtract_fusion
  317.1 0.3 fusion.29
  317.4 0.1 collective-permute-start
  317.5 1.3 copy-done
  318.8 0.3 copy-done.3
  319.1 1.8 fusion.7
  320.9 0.9 copy.58
  321.8 1.8 subtract_convert_fusion
  323.7 0.5 copy.42
  324.2 0.5 copy.43
  324.8 1.9 collective-permute-done
  326.7 0.0 copy-start.5
  326.7 8.2 %fusion.8 = f32[2,512,512,8]{2,1,3,0:T(8,128)} fusion(bf16[512,2,8,64]{3,0,2,1:T(8,128)(2,1)S(1)} %bitcast.124, bf16[512,2,8,64]{3,0,2,1:T(8,128)(2,1)S(1)} %bitcast.123, pred[]{:T(512)S(6)} %eq.43, bf16[512,4,128]{2,0,1:T(8,128)(2,1)S(1)} %fusion.29, s32[]{:T(128)S(6)} %select_n.70, bf16[512,4,128]{2,0,1:T(8,128)(2,1)S(1)} %collective-permute-done), kind=kOutput, calls=%fused_computation.18 | convolution fusion | flops 1078067200 | bytes 21495812 | tf_op jit(solution)/shard_map/tkgd,skd->kgts/dot_general | solution.py:154
  334.8 0.0 copy-done.5
  334.8 17.2 %fusion.69 = (f32[2,8,512]{2,1,0:T(8,128)S(1)}, f32[2,8,512,512]{2,3,1,0:T(8,128)}) fusion(f32[2,512,512,8]{2,1,3,0:T(8,128)} %fusion.8, pred[512,512]{0,1:T(8,128)(4,1)S(1)} %copy-done.5), kind=kOutput, calls=%fused_computation.93 | output fusion | flops 25166336 | bytes 33849344 | tf_op jit(solution)/shard_map/sub | solution.py:162
  352.1 7.2 %fusion.16 = bf16[2,128,8,512]{3,1,2,0:T(8,128)(2,1)S(1)} fusion(f32[2,8,512,512]{2,3,1,0:T(8,128)} %get-tuple-element.16, f32[2,8,512]{2,1,0:T(8,128)S(1)} %get-tuple-element.15, pred[]{:T(512)S(6)} %eq.43, bf16[512,4,128]{2,0,1:T(8,128)(2,1)S(1)} %fusion.29, s32[]{:T(128)S(6)} %select_n.70, bf16[512,4,128]{2,0,1:T(8,128)(2,1)S(1)} %collective-permute-done), kind=kOutput, calls=%fused_computation.26 | convolution fusion | flops 1083310080 | bytes 19431428 | tf_op jit(solution)/shard_map/kgts,skd->tkgd/dot_general | solution.py:165
  359.3 2.4 copy.46
  (6 shorter events, 0.0 us)
Async XLA Ops:
  3.2 10.2 %all-to-all-start.2 = ((bf16[4,64,512]{2,1,0:T(8,128)(2,1)}), bf16[4,64,512]{2,1,0:T(8,128)(2,1)S(1)}, u32[]{:S(2)}, u32[]{:S(2)}) async-start(bf16[4,64,512]{2,1,0:T(8,128)(2,1)} %copy.34), calls=%async_computation.2 | async-start | bytes 524288 | tf_op jit(solution)/shard_map/all_to_all | solution.py:80
  13.4 17.9 %all-to-all-start.3 = ((bf16[4,64,2048]{2,1,0:T(8,128)(2,1)}), bf16[4,64,2048]{2,1,0:T(8,128)(2,1)S(1)}, u32[]{:S(2)}, u32[]{:S(2)}) async-start(bf16[4,64,2048]{2,1,0:T(8,128)(2,1)} %copy.40), calls=%async_computation.3 | async-start | bytes 2097152 | tf_op jit(solution)/shard_map/all_to_all | solution.py:79
  31.4 33.6 %copy-start.4 = (bf16[4,64,2048]{2,1,0:T(8,128)(2,1)}, bf16[4,64,2048]{2,1,0:T(8,128)(2,1)S(1)}, u32[]{:S(2)}) copy-start(bf16[4,64,2048]{2,1,0:T(8,128)(2,1)S(1)} %all-to-all-done.3) | copy-start | bytes 3145732
  31.4 29.2 %copy-start.1 = (bf16[128,8192]{1,0:T(8,128)(2,1)S(1)}, bf16[128,8192]{1,0:T(8,128)(2,1)}, u32[]{:S(2)}) copy-start(bf16[128,8192]{1,0:T(8,128)(2,1)} %param.9) | copy-start | bytes 6291460
  64.9 6.0 %copy-start.6 = (s32[1,512]{1,0:T(1,128)S(1)}, s32[1,512]{1,0:T(1,128)}, u32[]{:S(2)}) copy-start(s32[1,512]{1,0:T(1,128)} %param.17) | copy-start | bytes 6148
  64.9 11.9 %copy-start.2 = (bf16[4,128,2048]{2,1,0:T(8,128)(2,1)S(1)}, bf16[4,128,2048]{2,1,0:T(8,128)(2,1)}, u32[]{:S(2)}) copy-start(bf16[4,128,2048]{2,1,0:T(8,128)(2,1)} %all_to_all.20) | copy-start | bytes 6291460
  64.9 189.5 %all-to-all-start = ((bf16[4,128,8192]{2,1,0:T(8,128)(2,1)}), bf16[4,128,8192]{2,1,0:T(8,128)(2,1)}, u32[]{:S(2)}, u32[]{:S(2)}) async-start(bf16[4,128,8192]{2,1,0:T(8,128)(2,1)} %stack.2), calls=%async_computation | async-start | bytes 16777216 | tf_op jit(solution)/shard_map/all_to_all | solution.py:98
  316.7 2.2 copy-start
  316.7 2.5 copy-start.3
  317.4 9.2 %collective-permute-start = (bf16[512,4,128]{2,0,1:T(8,128)(2,1)S(1)}, bf16[512,4,128]{2,0,1:T(8,128)(2,1)S(1)}, u32[]{:S(2)}, u32[]{:S(2)}) collective-permute-start(bf16[512,4,128]{2,0,1:T(8,128)(2,1)S(1)} %fusion.29), channel_id=1, source_target_pairs={{0,4},{4,0},{8,12},{12,8},{1,5},{5,1},{9,13},{13,9},{2,6},{6,2},{1... | collective-permute-start | bytes 1572872 | tf_op jit(solution)/shard_map/ppermute | solution.py:19
  326.7 8.2 %copy-start.5 = (pred[512,512]{0,1:T(8,128)(4,1)S(1)}, pred[512,512]{0,1:T(8,128)(4,1)}, u32[]{:S(2)}) copy-start(pred[512,512]{0,1:T(8,128)(4,1)} %fusion.31) | copy-start | bytes 786436
